TPU v7x, 128 devices: a whole 4x4x4 slice. The times are simulated.
128 devices in a mesh: sub: 16 (over x, y), row: 8 (over z, core).
Axes of the slice: x: 4, y: 4, z: 4, core: 2. Of those that a mesh axis runs over, the one named last changes fastest.
Arguments:
- sigma_top: float32 [6144, 6144], P('row', 'sub'), may hold values from -2 to 4, as said below
- coupling: float32 [16, 6144, 768], P('sub', 'row'), may hold values from -0.16 to 0.16
- child_inverse: float32 [16, 768, 768], P('sub', 'row'), may hold values from -1 to 10, as said below
- tile_mask: int32 [16, 24], P('sub'), may hold values 0 or 1
- obs_node: int32 [32768], P(('sub', 'row')), may hold values from 0 to 12287
- obs_noise: float32 [32768], P(('sub', 'row')), may hold values from 0.05 to 2
Outputs:
- sep_child: float32 [16, 6144, 768], P('sub', 'row')
- child_block: float32 [16, 768, 768], P('sub', 'row')
- loo_var: float32 [32768], P(('sub', 'row'))
Inputs may be any that keep to these rules, and one draw needn't show every extreme that they name: sigma_top is exactly symmetric. Each child_inverse[c] is exactly symmetric.
All inputs are finite; a program needn't handle non-finite values. No bound on the sum of `tile_mask` on one device may be relied on, other than what follows from the above.
Results may differ from a plain program's by a relative error of at most 0.000073.
Values sent between devices are 32-bit elements; how exact they have to be, the bound alone decides.
No kernel may reach another device: no remote copies, remote signals or barrier semaphores. Data moves between devices by JAX's collectives and lax.ppermute only.
A program may use at most 128 MiB of HBM per device.

v0:
```python
import jax
import jax.numpy as jnp
from jax import lax
from jax.sharding import PartitionSpec as P

TILE = 256


def local(sigma_top, coupling, child_inverse, tile_mask, obs_node, obs_noise):
    highest = lax.Precision.HIGHEST
    rows_here = coupling.shape[1]
    width_here = child_inverse.shape[1]
    tiles_here = rows_here // TILE
    row_index = lax.axis_index("row")
    mask_here = lax.dynamic_slice_in_dim(tile_mask[0], row_index * tiles_here, tiles_here)
    row_mask = jnp.repeat(mask_here, TILE).astype(jnp.float32)
    masked = coupling[0] * row_mask[:, None]
    gathered = lax.all_gather(masked, "row", axis=0, tiled=True)
    product = jnp.dot(
        lax.all_gather(sigma_top, "sub", axis=1, tiled=True),
        gathered,
        precision=highest,
        preferred_element_type=jnp.float32,
    )
    sep_part = -product
    update = lax.psum_scatter(
        lax.dot_general(
            masked,
            sep_part,
            (((0,), (0,)), ((), ())),
            precision=highest,
            preferred_element_type=jnp.float32,
        ),
        "row",
        scatter_dimension=0,
        tiled=True,
    )
    block_here = child_inverse[0] - update
    own_cols = lax.dynamic_slice_in_dim(block_here, row_index * width_here, width_here, 1)
    own_diag = jnp.diagonal(own_cols)
    every_var = lax.all_gather(own_diag, ("sub", "row"), axis=0, tiled=True)
    loo_var = every_var[obs_node] + obs_noise
    return (sep_part[None], block_here[None], loo_var)


def solution(mesh):
    placed = (
        P("row", "sub"),
        P("sub", "row", None),
        P("sub", "row", None),
        P("sub", None),
        P(("sub", "row")),
        P(("sub", "row")),
    )
    return jax.shard_map(
        local,
        mesh=mesh,
        in_specs=placed,
        out_specs=(P("sub", "row", None), P("sub", "row", None), P(("sub", "row"))),
        check_vma=False,
    )
```

profile of v0, /device:TPU:1, one launch (start us, length us, event | category | flops | bytes accessed | tf_op | source)
XLA Modules:
  0.0 450.1 jit_solution(1674996634150140336)
XLA Ops:
  7.2 0.0 all-gather.3.cloned.1.call-start
  7.2 0.7 convert_bitcast_fusion
  7.9 0.1 broadcast_in_dim.17
  8.0 3.3 bitcast_multiply_fusion
  11.3 0.0 all-gather.3.cloned.1.call-update
  11.3 0.0 all-gather.5.cloned.1.call-start
  11.4 0.7 all-gather.5.cloned.1.call-update
  12.1 0.0 copy-start
  12.1 0.0 reduce-scatter.2.cloned.1.call-start
  12.2 97.0 %all-gather.3.cloned.1.call-done = f32[6144,768]{1,0:T(8,128)} async-done(((f32[768,768]{1,0:T(8,128)}), f32[6144,768]{1,0:T(8,128)}) %all-gather.3.cloned.1.call-update) | async-done | bytes 18874384 | tf_op jit(solution)/shard_map/all_gather | solution.py:18
  109.1 124.2 %all-gather.5.cloned.1.call-done = f32[768,6144]{1,0:T(8,128)} async-done(((f32[768,384]{1,0:T(8,128)}), f32[768,6144]{1,0:T(8,128)}) %all-gather.5.cloned.1.call-update) | async-done | bytes 18874384 | tf_op jit(solution)/shard_map/all_gather | solution.py:20
  233.4 92.2 %fusion.2 = f32[768,768]{1,0:T(8,128)S(1)} fusion(f32[6144,768]{1,0:T(8,128)} %all-gather.3.cloned.1.call-done, f32[768,6144]{1,0:T(8,128)} %all-gather.5.cloned.1.call-done), kind=kOutput, calls=%fused_computation.12 | convolution fusion | flops 43486543872 | bytes 40108032 | tf_op jit(solution)/shard_map/dot_general | solution.py:19
  325.5 0.0 copy-start.1
  325.5 1.4 copy-done.1
  326.9 0.0 copy-done
  326.9 12.5 %fusion = f32[768,768]{1,0:T(8,128)} fusion(f32[768,768]{1,0:T(8,128)S(1)} %copy-done, f32[768,768]{1,0:T(8,128)S(1)} %fusion.2), kind=kOutput, calls=%fused_computation.3 | convolution fusion | flops 5436407808 | bytes 7077888 | tf_op jit(solution)/shard_map/dot_general | solution.py:27
  339.5 0.0 copy-start.6
  339.5 0.0 copy-start.2
  339.5 0.0 reduce-scatter.2.cloned.1.call-update
  339.5 0.6 copy-done.6
  340.2 1.0 copy-done.2
  341.2 1.6 negate_bitcast_fusion
  342.7 0.0 copy-start.4
  342.7 3.1 copy.10
  345.8 0.0 copy-start.5
  345.8 24.8 %reduce-scatter.2.cloned.1.call-done = f32[96,768]{1,0:T(8,128)} async-done(((f32[768,768]{1,0:T(8,128)}), f32[96,768]{1,0:T(8,128)}) %reduce-scatter.2.cloned.1.call-update) | async-done | bytes 294928 | tf_op jit(solution)/shard_map/reduce_scatter | solution.py:26
  370.6 0.0 copy-done.4
  370.6 1.0 bitcast_subtract_fusion
  371.6 0.0 copy-start.3
  371.6 0.1 constant_dynamic-slice_fusion
  371.7 1.2 gather_fusion
  373.0 0.3 dynamic-update-slice
  373.2 68.1 %all-reduce = f32[12288]{0:T(1024)S(1)} all-reduce(f32[12288]{0:T(1024)S(1)} %dynamic-update-slice), channel_id=1, replica_groups=mesh['sub'=16,'row'=8] {'sub','row'}, use_global_device_ids=true, to_apply=%add | all-reduce | flops 12288 | bytes 98304
  441.3 1.7 gather_fusion.1
  443.0 0.0 copy-done.5
  443.1 0.6 add.25
  443.6 0.0 copy-done.3
  (5 shorter events, 0.0 us)
Async XLA Ops:
  7.2 102.0 %all-gather.3.cloned.1.call-start = ((), (), s32[]{:S(2)}) async-start(), calls=%async_computation.1 | async-start | bytes 21233664 | tf_op jit(solution)/shard_map/all_gather | solution.py:18
  11.3 222.0 %all-gather.5.cloned.1.call-start = ((), (), s32[]{:S(2)}) async-start(), calls=%async_computation.2 | async-start | bytes 20054016 | tf_op jit(solution)/shard_map/all_gather | solution.py:20
  12.1 314.8 %copy-start = (f32[768,768]{1,0:T(8,128)S(1)}, f32[768,768]{1,0:T(8,128)}, u32[]{:S(2)}) copy-start(f32[768,768]{1,0:T(8,128)} %bitcast_multiply_fusion) | copy-start | bytes 7077892
  12.1 358.5 %reduce-scatter.2.cloned.1.call-start = ((), (), s32[]{:S(2)}) async-start(), calls=%async_computation.3 | async-start | bytes 2654208 | tf_op jit(solution)/shard_map/reduce_scatter | solution.py:26
  325.5 1.4 copy-start.1
  339.5 0.7 copy-start.6
  339.5 1.7 copy-start.2
  342.7 27.9 %copy-start.4 = (f32[1,96,768]{2,1,0:T(8,128)S(1)}, f32[1,96,768]{2,1,0:T(8,128)}, u32[]{:S(2)}) copy-start(f32[1,96,768]{2,1,0:T(8,128)} %param.8) | copy-start | bytes 884740
  345.8 97.2 %copy-start.5 = (f32[256]{0:T(256)S(1)}, f32[256]{0:T(256)}, u32[]{:S(2)}) copy-start(f32[256]{0:T(256)} %param.11) | copy-start | bytes 3076
  371.6 72.0 %copy-start.3 = (f32[96,768]{1,0:T(8,128)}, f32[96,768]{1,0:T(8,128)S(1)}, u32[]{:S(2)}) copy-start(f32[96,768]{1,0:T(8,128)S(1)} %bitcast_subtract_fusion) | copy-start | bytes 884740
Sparse Core Ops, SparseCore 0:
  11.5 97.6 all-gather.2
  111.3 121.9 all-gather.4
  339.6 30.9 reduce-scatter.1
where the time goes:
time: 450 us
  waiting for transfers between devices  247 us (55%)
  matrix products  105 us (23%)
  blocking collectives  68.1 us (15%)
  between operations  13.8 us (3%)
  local copies, waits for them, and re-layouts  9.55 us (2%)
  other arithmetic  7.17 us (2%)
    all_gather x1, waiting for transfers between devices, local(): lax.all_gather(sigma_top, 'sub', axis=1, tiled=True)  124 us
    all_gather x1, waiting for transfers between devices, local(): gathered = lax.all_gather(masked, 'row', axis=0, tiled=True)  97 us
    dot_general x1, matrix products, local(): jnp.dot(lax.all_gather(sigma_top, 'sub', axis=1, tiled=True), gathered, p...  92.2 us
    unnamed x1, blocking collectives  68.1 us
    reduce_scatter x1, waiting for transfers between devices, local(): lax.psum_scatter(lax.dot_general(masked, sep_part, (((0,), (0,)), ((), ()...  24.8 us
    dot_general x1, matrix products, local(): lax.dot_general(masked, sep_part, (((0,), (0,)), ((), ())), precision=hig...  12.5 us
  transfers between devices with their start and end apart: 3, of which 3 were waited for; matrix products, arithmetic and copies ran while one was open for 1% of the time, Pallas kernels for 0%

commit v1 on v0

--- a/solution.py
+++ b/solution.py
@@ -4,6 +4,22 @@
 from jax.sharding import PartitionSpec as P
 
 TILE = 256
+
+
+def ring_gather(x, axis, dim):
+    ways, here, hop = (lax.axis_size(axis), lax.axis_index(axis), x.shape[dim])
+    lengths = [n * ways if d == dim else n for d, n in enumerate(x.shape)]
+    full = lax.dynamic_update_slice_in_dim(jnp.zeros(lengths, x.dtype), x, here * hop, axis=dim)
+    going_up = going_down = x
+    for far in range(1, ways // 2 + 1):
+        going_up = lax.ppermute(going_up, axis, [(d, (d + 1) % ways) for d in range(ways)])
+        full = lax.dynamic_update_slice_in_dim(full, going_up, (here - far) % ways * hop, axis=dim)
+        if 2 * far < ways:
+            going_down = lax.ppermute(going_down, axis, [(d, (d - 1) % ways) for d in range(ways)])
+            full = lax.dynamic_update_slice_in_dim(
+                full, going_down, (here + far) % ways * hop, axis=dim
+            )
+    return full
 
 
 def local(sigma_top, coupling, child_inverse, tile_mask, obs_node, obs_noise):
@@ -17,7 +33,7 @@
     masked = coupling[0] * row_mask[:, None]
     gathered = lax.all_gather(masked, "row", axis=0, tiled=True)
     product = jnp.dot(
-        lax.all_gather(sigma_top, "sub", axis=1, tiled=True),
+        ring_gather(sigma_top, "sub", 1),
         gathered,
         precision=highest,
         preferred_element_type=jnp.float32,

time: 450 us -> 407 us (0.904)
  waiting for transfers between devices: 247 us -> 185 us
  matrix products: 105 us -> 57.5 us
  starting transfers between devices: 0.12 us -> 32.8 us
  local copies, waits for them, and re-layouts: 9.55 us -> 39.3 us
    ppermute x0 -> x15, waiting for transfers between devices: none -> 153 us  [the longest x8 153 us: ring_gather(): lax.ppermute(going_up, axis, [(d, (d + 1) % ways) for d in range(ways)])]
    all_gather x1 -> x0, waiting for transfers between devices: 124 us -> none  [local(): lax.all_gather(sigma_top, 'sub', axis=1, tiled=True)]
    all_gather x1, waiting for transfers between devices: 97 us -> 0.02 us  [local(): gathered = lax.all_gather(masked, 'row', axis=0, tiled=True)]
    dot_general x1, matrix products: 92.2 us -> 49.7 us  [local(): jnp.dot(ring_gather(sigma_top, 'sub', 1), gathered, precision=highest, pr...]
    ppermute x0 -> x15, starting transfers between devices: none -> 32.7 us  [the longest x7 30.5 us: ring_gather(): lax.ppermute(going_down, axis, [(d, (d - 1) % ways) for d in range(ways)])]
    dynamic_update_slice x0 -> x16, local copies, waits for them, and re-layouts: none -> 23.5 us  [the longest x8 11.8 us: ring_gather(): lax.dynamic_update_slice_in_dim(full, going_up, (here - far) % ways * hop...]
    broadcast_in_dim x0 -> x1, local copies, waits for them, and re-layouts: none -> 8.81 us  [ring_gather(): jnp.zeros(lengths, x.dtype)]
    reduce_scatter x1, waiting for transfers between devices: 24.8 us -> 31.7 us  [local(): lax.psum_scatter(lax.dot_general(masked, sep_part, (((0,), (0,)), ((), ()...]
  transfers between devices with their start and end apart: 3 -> 17, of which waited for: 3 -> 9; matrix products, arithmetic and copies ran while one was open for 1% -> 9% of each run, Pallas kernels for 0% -> 0%
where the time goes in v1:
time: 407 us; the launch traced here: 406 us
  waiting for transfers between devices  185 us (45%)
  blocking collectives  68.1 us (17%)
  matrix products  57.5 us (14%)
  local copies, waits for them, and re-layouts  39.3 us (10%)
  starting transfers between devices  32.8 us (8%)
  between operations  14.3 us (4%)
  other arithmetic  8.92 us (2%)
    ppermute x8, waiting for transfers between devices, ring_gather(): lax.ppermute(going_up, axis, [(d, (d + 1) % ways) for d in range(ways)])  153 us
    unnamed x1, blocking collectives  68.1 us
    dot_general x1, matrix products, local(): jnp.dot(ring_gather(sigma_top, 'sub', 1), gathered, precision=highest, pr...  49.7 us
    reduce_scatter x1, waiting for transfers between devices, local(): lax.psum_scatter(lax.dot_general(masked, sep_part, (((0,), (0,)), ((), ()...  31.7 us
    ppermute x7, starting transfers between devices, ring_gather(): lax.ppermute(going_down, axis, [(d, (d - 1) % ways) for d in range(ways)])  30.5 us
    dynamic_update_slice x8, local copies, waits for them, and re-layouts, ring_gather(): lax.dynamic_update_slice_in_dim(full, going_up, (here - far) % ways * hop...  11.8 us
    dynamic_update_slice x7, local copies, waits for them, and re-layouts, ring_gather(): lax.dynamic_update_slice_in_dim(full, going_down, (here + far) % ways * h...  10.5 us
    broadcast_in_dim x1, local copies, waits for them, and re-layouts, ring_gather(): jnp.zeros(lengths, x.dtype)  8.81 us
  transfers between devices with their start and end apart: 17, of which 9 were waited for; matrix products, arithmetic and copies ran while one was open for 9% of the time, Pallas kernels for 0%

profile of v1, /device:TPU:1, one launch (start us, length us, event | category | flops | bytes accessed | tf_op | source)
XLA Modules:
  0.0 406.1 jit_solution(12621685151519099545)
XLA Ops:
  7.2 0.0 copy-start.2
  7.2 0.0 all-gather.2.cloned.1.call-start
  7.2 0.8 fusion.3
  8.0 0.1 broadcast_in_dim.21
  8.1 3.3 bitcast_multiply_fusion
  11.4 0.0 all-gather.2.cloned.1.call-update
  11.4 0.0 reduce-scatter.2.cloned.1.call-start
  11.5 2.2 collective-permute-start
  13.7 3.7 collective-permute-start.1
  17.4 25.8 %collective-permute-done = f32[768,384]{1,0:T(8,128)S(1)} collective-permute-done((f32[768,384]{1,0:T(8,128)}, f32[768,384]{1,0:T(8,128)S(1)}, u32[]{:S(2)}, u32[]{:S(2)}) %collective-permute-start) | collective-permute-done | bytes 1179680 | tf_op jit(solution)/shard_map/ppermute | solution.py:15
  43.2 4.8 %collective-permute-start.3 = (f32[768,384]{1,0:T(8,128)S(1)}, f32[768,384]{1,0:T(8,128)S(1)}, u32[]{:S(2)}, u32[]{:S(2)}) collective-permute-start(f32[768,384]{1,0:T(8,128)S(1)} %collective-permute-done.1), channel_id=1, source_target_pairs={{0,120},{8,0},{16,8},{24,16},{32,24},{40,32},{48,40},{56,48},{64,5... | collective-permute-start | bytes 3538952 | tf_op jit(solution)/shard_map/ppermute | solution.py:18
  48.0 24.7 %collective-permute-done.2 = f32[768,384]{1,0:T(8,128)S(1)} collective-permute-done((f32[768,384]{1,0:T(8,128)S(1)}, f32[768,384]{1,0:T(8,128)S(1)}, u32[]{:S(2)}, u32[]{:S(2)}) %collective-permute-start.2) | collective-permute-done | bytes 1179680 | tf_op jit(solution)/shard_map/ppermute | solution.py:15
  72.7 0.0 collective-permute-start.4
  72.7 0.0 collective-permute-done.3
  72.7 4.8 %collective-permute-start.5 = (f32[768,384]{1,0:T(8,128)S(1)}, f32[768,384]{1,0:T(8,128)S(1)}, u32[]{:S(2)}, u32[]{:S(2)}) collective-permute-start(f32[768,384]{1,0:T(8,128)S(1)} %collective-permute-done.3), channel_id=1, source_target_pairs={{0,120},{8,0},{16,8},{24,16},{32,24},{40,32},{48,40},{56,48},{64,5... | collective-permute-start | bytes 3538952 | tf_op jit(solution)/shard_map/ppermute | solution.py:18
  77.5 23.7 %collective-permute-done.4 = f32[768,384]{1,0:T(8,128)S(1)} collective-permute-done((f32[768,384]{1,0:T(8,128)S(1)}, f32[768,384]{1,0:T(8,128)S(1)}, u32[]{:S(2)}, u32[]{:S(2)}) %collective-permute-start.4) | collective-permute-done | bytes 1179680 | tf_op jit(solution)/shard_map/ppermute | solution.py:15
  101.3 4.8 %collective-permute-start.7 = (f32[768,384]{1,0:T(8,128)S(1)}, f32[768,384]{1,0:T(8,128)S(1)}, u32[]{:S(2)}, u32[]{:S(2)}) collective-permute-start(f32[768,384]{1,0:T(8,128)S(1)} %collective-permute-done.5), channel_id=1, source_target_pairs={{0,120},{8,0},{16,8},{24,16},{32,24},{40,32},{48,40},{56,48},{64,5... | collective-permute-start | bytes 3538952 | tf_op jit(solution)/shard_map/ppermute | solution.py:18
  106.0 22.9 %collective-permute-done.6 = f32[768,384]{1,0:T(8,128)S(1)} collective-permute-done((f32[768,384]{1,0:T(8,128)S(1)}, f32[768,384]{1,0:T(8,128)S(1)}, u32[]{:S(2)}, u32[]{:S(2)}) %collective-permute-start.6) | collective-permute-done | bytes 1179680 | tf_op jit(solution)/shard_map/ppermute | solution.py:15
  128.9 0.0 collective-permute-start.8
  128.9 1.0 copy-done.5
  129.9 3.8 collective-permute-start.9
  133.8 21.9 %collective-permute-done.8 = f32[768,384]{1,0:T(8,128)S(1)} collective-permute-done((f32[768,384]{1,0:T(8,128)S(1)}, f32[768,384]{1,0:T(8,128)S(1)}, u32[]{:S(2)}, u32[]{:S(2)}) %collective-permute-start.8) | collective-permute-done | bytes 1179680 | tf_op jit(solution)/shard_map/ppermute | solution.py:15
  155.6 0.0 collective-permute-start.10
  155.7 1.1 copy-done.15
  156.7 3.8 collective-permute-start.11
  160.5 21.0 %collective-permute-done.10 = f32[768,384]{1,0:T(8,128)} collective-permute-done((f32[768,384]{1,0:T(8,128)S(1)}, f32[768,384]{1,0:T(8,128)}, u32[]{:S(2)}, u32[]{:S(2)}) %collective-permute-start.10) | collective-permute-done | bytes 1179680 | tf_op jit(solution)/shard_map/ppermute | solution.py:15
  181.6 0.0 collective-permute-start.12
  181.6 8.8 %broadcast_in_dim.20 = f32[768,6144]{1,0:T(8,128)} broadcast(f32[]{:T(128)} %constant.103.clone.1), dimensions={} | broadcast | bytes 18874372 | tf_op jit(solution)/shard_map/broadcast_in_dim | solution.py:12
  190.4 1.2 constant_dynamic-update-slice_fusion.15
  191.6 1.2 constant_dynamic-update-slice_fusion.14
  192.8 1.2 constant_dynamic-update-slice_fusion.13
  194.0 1.2 constant_dynamic-update-slice_fusion.12
  195.1 1.1 constant_dynamic-update-slice_fusion.11
  196.2 0.0 collective-permute-done.11
  196.3 4.8 %collective-permute-start.13 = (f32[768,384]{1,0:T(8,128)}, f32[768,384]{1,0:T(8,128)S(1)}, u32[]{:S(2)}, u32[]{:S(2)}) collective-permute-start(f32[768,384]{1,0:T(8,128)} %collective-permute-done.11), channel_id=1, source_target_pairs={{0,120},{8,0},{16,8},{24,16},{32,24},{40,32},{48,40},{56,48},{64,5... | collective-permute-start | bytes 3538952 | tf_op jit(solution)/shard_map/ppermute | solution.py:18
  201.1 1.1 constant_dynamic-update-slice_fusion.10
  202.2 4.6 %collective-permute-done.12 = f32[768,384]{1,0:T(8,128)} collective-permute-done((f32[768,384]{1,0:T(8,128)}, f32[768,384]{1,0:T(8,128)}, u32[]{:S(2)}, u32[]{:S(2)}) %collective-permute-start.12) | collective-permute-done | bytes 1179680 | tf_op jit(solution)/shard_map/ppermute | solution.py:15
  206.8 0.0 collective-permute-start.14
  206.8 1.1 constant_dynamic-update-slice_fusion.9
  207.9 1.1 constant_dynamic-update-slice_fusion.8
  209.0 1.1 constant_dynamic-update-slice_fusion.7
  210.2 1.2 constant_dynamic-update-slice_fusion.6
  211.3 2.4 constant_dynamic-update-slice_fusion.5
  213.8 2.4 constant_dynamic-update-slice_fusion.4
  216.2 2.4 constant_dynamic-update-slice_fusion.3
  218.6 2.4 constant_dynamic-update-slice_fusion.2
  221.0 1.2 constant_dynamic-update-slice_fusion.1
  222.2 8.9 %collective-permute-done.14 = f32[768,384]{1,0:T(8,128)S(1)} collective-permute-done((f32[768,384]{1,0:T(8,128)}, f32[768,384]{1,0:T(8,128)S(1)}, u32[]{:S(2)}, u32[]{:S(2)}) %collective-permute-start.14) | collective-permute-done | bytes 1179680 | tf_op jit(solution)/shard_map/ppermute | solution.py:15
  231.1 1.1 constant_dynamic-update-slice_fusion
  232.2 0.0 all-gather.2.cloned.1.call-done
  232.3 49.7 %fusion.4 = f32[768,768]{1,0:T(8,128)S(1)} fusion(f32[768,6144]{1,0:T(8,128)} %constant_dynamic-update-slice_fusion, f32[6144,768]{1,0:T(8,128)} %all-gather.2.cloned.1.call-done), kind=kOutput, calls=%fused_computation.30 | convolution fusion | flops 43486543872 | bytes 40108032 | tf_op jit(solution)/shard_map/dot_general | solution.py:35
  282.0 1.4 copy-done.1
  283.4 7.7 %fusion = f32[768,768]{1,0:T(8,128)} fusion(f32[768,768]{1,0:T(8,128)S(1)} %copy-done, f32[768,768]{1,0:T(8,128)S(1)} %fusion.4), kind=kOutput, calls=%fused_computation.3 | convolution fusion | flops 5436407808 | bytes 7077888 | tf_op jit(solution)/shard_map/dot_general | solution.py:43
  291.2 0.0 reduce-scatter.2.cloned.1.call-update
  291.2 3.2 negate_bitcast_fusion
  294.5 31.7 %reduce-scatter.2.cloned.1.call-done = f32[96,768]{1,0:T(8,128)} async-done(((f32[768,768]{1,0:T(8,128)}), f32[96,768]{1,0:T(8,128)}) %reduce-scatter.2.cloned.1.call-update) | async-done | bytes 294928 | tf_op jit(solution)/shard_map/reduce_scatter | solution.py:42
  326.2 1.0 bitcast_subtract_fusion
  327.2 0.0 copy-start.17
  327.2 0.1 constant_dynamic-slice_fusion
  327.3 1.2 gather_fusion
  328.6 0.3 dynamic-update-slice
  328.9 68.1 %all-reduce = f32[12288]{0:T(1024)S(1)} all-reduce(f32[12288]{0:T(1024)S(1)} %dynamic-update-slice), channel_id=1, replica_groups=mesh['sub'=16,'row'=8] {'sub','row'}, use_global_device_ids=true, to_apply=%add | all-reduce | flops 12288 | bytes 98304
  396.9 1.7 gather_fusion.1
  398.7 0.6 add.186
  (49 shorter events, 0.1 us)
Async XLA Ops:
  7.2 183.3 %copy-start.2 = (f32[768,384]{1,0:T(8,128)S(1)}, f32[768,384]{1,0:T(8,128)}, u32[]{:S(2)}) copy-start(f32[768,384]{1,0:T(8,128)} %param.6) | copy-start | bytes 3538948
  7.2 225.1 %all-gather.2.cloned.1.call-start = ((), (), s32[]{:S(2)}) async-start(), calls=%async_computation.1 | async-start | bytes 21233664 | tf_op jit(solution)/shard_map/all_gather | solution.py:34
  11.4 314.8 %reduce-scatter.2.cloned.1.call-start = ((), (), s32[]{:S(2)}) async-start(), calls=%async_computation.2 | async-start | bytes 2654208 | tf_op jit(solution)/shard_map/reduce_scatter | solution.py:42
  11.5 31.7 %collective-permute-start = (f32[768,384]{1,0:T(8,128)}, f32[768,384]{1,0:T(8,128)S(1)}, u32[]{:S(2)}, u32[]{:S(2)}) collective-permute-start(f32[768,384]{1,0:T(8,128)} %param.6), channel_id=1, source_target_pairs={{0,8},{8,16},{16,24},{24,32},{32,40},{40,48},{48,56},{56,64},{64,7... | collective-permute-start | bytes 3538952 | tf_op jit(solution)/shard_map/ppermute | solution.py:15
  13.7 29.5 %collective-permute-start.1 = (f32[768,384]{1,0:T(8,128)}, f32[768,384]{1,0:T(8,128)S(1)}, u32[]{:S(2)}, u32[]{:S(2)}) collective-permute-start(f32[768,384]{1,0:T(8,128)} %param.6), channel_id=1, source_target_pairs={{0,120},{8,0},{16,8},{24,16},{32,24},{40,32},{48,40},{56,48},{64,5... | collective-permute-start | bytes 3538952 | tf_op jit(solution)/shard_map/ppermute | solution.py:18
  43.2 29.5 %collective-permute-start.2 = (f32[768,384]{1,0:T(8,128)S(1)}, f32[768,384]{1,0:T(8,128)S(1)}, u32[]{:S(2)}, u32[]{:S(2)}) collective-permute-start(f32[768,384]{1,0:T(8,128)S(1)} %collective-permute-done), channel_id=1, source_target_pairs={{0,8},{8,16},{16,24},{24,32},{32,40},{40,48},{48,56},{56,64},{64,7... | collective-permute-start | bytes 3538952 | tf_op jit(solution)/shard_map/ppermute | solution.py:15
  43.2 29.5 %copy-start.3 = (f32[768,384]{1,0:T(8,128)}, f32[768,384]{1,0:T(8,128)S(1)}, u32[]{:S(2)}) copy-start(f32[768,384]{1,0:T(8,128)S(1)} %collective-permute-done.1) | copy-start | bytes 3538948
  43.2 29.5 %collective-permute-start.3 = (f32[768,384]{1,0:T(8,128)S(1)}, f32[768,384]{1,0:T(8,128)S(1)}, u32[]{:S(2)}, u32[]{:S(2)}) collective-permute-start(f32[768,384]{1,0:T(8,128)S(1)} %collective-permute-done.1), channel_id=1, source_target_pairs={{0,120},{8,0},{16,8},{24,16},{32,24},{40,32},{48,40},{56,48},{64,5... | collective-permute-start | bytes 3538952 | tf_op jit(solution)/shard_map/ppermute | solution.py:18
  72.7 4.9 %copy-start.9 = (f32[768,384]{1,0:T(8,128)}, f32[768,384]{1,0:T(8,128)S(1)}, u32[]{:S(2)}) copy-start(f32[768,384]{1,0:T(8,128)S(1)} %collective-permute-done.2) | copy-start | bytes 3538948
  72.7 28.6 %collective-permute-start.4 = (f32[768,384]{1,0:T(8,128)S(1)}, f32[768,384]{1,0:T(8,128)S(1)}, u32[]{:S(2)}, u32[]{:S(2)}) collective-permute-start(f32[768,384]{1,0:T(8,128)S(1)} %collective-permute-done.2), channel_id=1, source_target_pairs={{0,8},{8,16},{16,24},{24,32},{32,40},{40,48},{48,56},{56,64},{64,7... | collective-permute-start | bytes 3538952 | tf_op jit(solution)/shard_map/ppermute | solution.py:15
  72.7 28.6 %copy-start.13 = (f32[768,384]{1,0:T(8,128)}, f32[768,384]{1,0:T(8,128)S(1)}, u32[]{:S(2)}) copy-start(f32[768,384]{1,0:T(8,128)S(1)} %collective-permute-done.3) | copy-start | bytes 3538948
  72.7 28.6 %collective-permute-start.5 = (f32[768,384]{1,0:T(8,128)S(1)}, f32[768,384]{1,0:T(8,128)S(1)}, u32[]{:S(2)}, u32[]{:S(2)}) collective-permute-start(f32[768,384]{1,0:T(8,128)S(1)} %collective-permute-done.3), channel_id=1, source_target_pairs={{0,120},{8,0},{16,8},{24,16},{32,24},{40,32},{48,40},{56,48},{64,5... | collective-permute-start | bytes 3538952 | tf_op jit(solution)/shard_map/ppermute | solution.py:18
  101.2 54.4 %copy-start.7 = (f32[768,384]{1,0:T(8,128)}, f32[768,384]{1,0:T(8,128)S(1)}, u32[]{:S(2)}) copy-start(f32[768,384]{1,0:T(8,128)S(1)} %collective-permute-done.4) | copy-start | bytes 3538948
  101.2 27.7 %collective-permute-start.6 = (f32[768,384]{1,0:T(8,128)S(1)}, f32[768,384]{1,0:T(8,128)S(1)}, u32[]{:S(2)}, u32[]{:S(2)}) collective-permute-start(f32[768,384]{1,0:T(8,128)S(1)} %collective-permute-done.4), channel_id=1, source_target_pairs={{0,8},{8,16},{16,24},{24,32},{32,40},{40,48},{48,56},{56,64},{64,7... | collective-permute-start | bytes 3538952 | tf_op jit(solution)/shard_map/ppermute | solution.py:15
  101.3 27.6 %collective-permute-start.7 = (f32[768,384]{1,0:T(8,128)S(1)}, f32[768,384]{1,0:T(8,128)S(1)}, u32[]{:S(2)}, u32[]{:S(2)}) collective-permute-start(f32[768,384]{1,0:T(8,128)S(1)} %collective-permute-done.5), channel_id=1, source_target_pairs={{0,120},{8,0},{16,8},{24,16},{32,24},{40,32},{48,40},{56,48},{64,5... | collective-permute-start | bytes 3538952 | tf_op jit(solution)/shard_map/ppermute | solution.py:18
  128.9 1.0 copy-start.5
  128.9 26.7 %collective-permute-start.8 = (f32[768,384]{1,0:T(8,128)S(1)}, f32[768,384]{1,0:T(8,128)S(1)}, u32[]{:S(2)}, u32[]{:S(2)}) collective-permute-start(f32[768,384]{1,0:T(8,128)S(1)} %collective-permute-done.6), channel_id=1, source_target_pairs={{0,8},{8,16},{16,24},{24,32},{32,40},{40,48},{48,56},{56,64},{64,7... | collective-permute-start | bytes 3538952 | tf_op jit(solution)/shard_map/ppermute | solution.py:15
  129.9 25.7 %copy-start.11 = (f32[768,384]{1,0:T(8,128)}, f32[768,384]{1,0:T(8,128)S(1)}, u32[]{:S(2)}) copy-start(f32[768,384]{1,0:T(8,128)S(1)} %collective-permute-done.7) | copy-start | bytes 3538948
  129.9 25.7 %collective-permute-start.9 = (f32[768,384]{1,0:T(8,128)S(1)}, f32[768,384]{1,0:T(8,128)}, u32[]{:S(2)}, u32[]{:S(2)}) collective-permute-start(f32[768,384]{1,0:T(8,128)S(1)} %collective-permute-done.7), channel_id=1, source_target_pairs={{0,120},{8,0},{16,8},{24,16},{32,24},{40,32},{48,40},{56,48},{64,5... | collective-permute-start | bytes 3538952 | tf_op jit(solution)/shard_map/ppermute | solution.py:18
  155.6 1.1 copy-start.15
  155.6 25.9 %collective-permute-start.10 = (f32[768,384]{1,0:T(8,128)S(1)}, f32[768,384]{1,0:T(8,128)}, u32[]{:S(2)}, u32[]{:S(2)}) collective-permute-start(f32[768,384]{1,0:T(8,128)S(1)} %collective-permute-done.8), channel_id=1, source_target_pairs={{0,8},{8,16},{16,24},{24,32},{32,40},{40,48},{48,56},{56,64},{64,7... | collective-permute-start | bytes 3538952 | tf_op jit(solution)/shard_map/ppermute | solution.py:15
  156.7 39.5 %collective-permute-start.11 = (f32[768,384]{1,0:T(8,128)}, f32[768,384]{1,0:T(8,128)}, u32[]{:S(2)}, u32[]{:S(2)}) collective-permute-start(f32[768,384]{1,0:T(8,128)} %collective-permute-done.9), channel_id=1, source_target_pairs={{0,120},{8,0},{16,8},{24,16},{32,24},{40,32},{48,40},{56,48},{64,5... | collective-permute-start | bytes 3538952 | tf_op jit(solution)/shard_map/ppermute | solution.py:18
  181.6 25.2 %collective-permute-start.12 = (f32[768,384]{1,0:T(8,128)}, f32[768,384]{1,0:T(8,128)}, u32[]{:S(2)}, u32[]{:S(2)}) collective-permute-start(f32[768,384]{1,0:T(8,128)} %collective-permute-done.10), channel_id=1, source_target_pairs={{0,8},{8,16},{16,24},{24,32},{32,40},{40,48},{48,56},{56,64},{64,7... | collective-permute-start | bytes 3538952 | tf_op jit(solution)/shard_map/ppermute | solution.py:15
  181.6 11.2 %copy-start.4 = (f32[768,384]{1,0:T(8,128)S(1)}, f32[768,384]{1,0:T(8,128)}, u32[]{:S(2)}) copy-start(f32[768,384]{1,0:T(8,128)} %copy-done.3) | copy-start | bytes 3538948
  181.6 12.4 %copy-start.10 = (f32[768,384]{1,0:T(8,128)S(1)}, f32[768,384]{1,0:T(8,128)}, u32[]{:S(2)}) copy-start(f32[768,384]{1,0:T(8,128)} %copy-done.9) | copy-start | bytes 3538948
  181.6 13.6 %copy-start.14 = (f32[768,384]{1,0:T(8,128)S(1)}, f32[768,384]{1,0:T(8,128)}, u32[]{:S(2)}) copy-start(f32[768,384]{1,0:T(8,128)} %copy-done.13) | copy-start | bytes 3538948
  181.6 19.5 %copy-start.8 = (f32[768,384]{1,0:T(8,128)S(1)}, f32[768,384]{1,0:T(8,128)}, u32[]{:S(2)}) copy-start(f32[768,384]{1,0:T(8,128)} %copy-done.7) | copy-start | bytes 3538948
  181.6 26.3 %copy-start.6 = (f32[768,384]{1,0:T(8,128)S(1)}, f32[768,384]{1,0:T(8,128)}, u32[]{:S(2)}) copy-start(f32[768,384]{1,0:T(8,128)} %copy-done.5) | copy-start | bytes 3538948
  181.6 27.4 %copy-start.12 = (f32[768,384]{1,0:T(8,128)S(1)}, f32[768,384]{1,0:T(8,128)}, u32[]{:S(2)}) copy-start(f32[768,384]{1,0:T(8,128)} %copy-done.11) | copy-start | bytes 3538948
  181.6 28.6 %copy-start.16 = (f32[768,384]{1,0:T(8,128)S(1)}, f32[768,384]{1,0:T(8,128)}, u32[]{:S(2)}) copy-start(f32[768,384]{1,0:T(8,128)} %copy-done.15) | copy-start | bytes 3538948
  196.3 24.8 %collective-permute-start.13 = (f32[768,384]{1,0:T(8,128)}, f32[768,384]{1,0:T(8,128)S(1)}, u32[]{:S(2)}, u32[]{:S(2)}) collective-permute-start(f32[768,384]{1,0:T(8,128)} %collective-permute-done.11), channel_id=1, source_target_pairs={{0,120},{8,0},{16,8},{24,16},{32,24},{40,32},{48,40},{56,48},{64,5... | collective-permute-start | bytes 3538952 | tf_op jit(solution)/shard_map/ppermute | solution.py:18
  206.8 24.3 %collective-permute-start.14 = (f32[768,384]{1,0:T(8,128)}, f32[768,384]{1,0:T(8,128)S(1)}, u32[]{:S(2)}, u32[]{:S(2)}) collective-permute-start(f32[768,384]{1,0:T(8,128)} %collective-permute-done.12), channel_id=1, source_target_pairs={{0,8},{8,16},{16,24},{24,32},{32,40},{40,48},{48,56},{56,64},{64,7... | collective-permute-start | bytes 3538952 | tf_op jit(solution)/shard_map/ppermute | solution.py:15
  232.2 51.2 %copy-start = (f32[768,768]{1,0:T(8,128)S(1)}, f32[768,768]{1,0:T(8,128)}, u32[]{:S(2)}) copy-start(f32[768,768]{1,0:T(8,128)} %bitcast_multiply_fusion) | copy-start | bytes 7077892
  232.2 59.0 %copy-start.20 = (s32[256]{0:T(256)S(1)}, s32[256]{0:T(256)}, u32[]{:S(2)}) copy-start(s32[256]{0:T(256)} %param.10) | copy-start | bytes 3076
  232.2 94.0 %copy-start.18 = (f32[1,96,768]{2,1,0:T(8,128)S(1)}, f32[1,96,768]{2,1,0:T(8,128)}, u32[]{:S(2)}) copy-start(f32[1,96,768]{2,1,0:T(8,128)} %param.8) | copy-start | bytes 884740
  232.2 166.4 %copy-start.19 = (f32[256]{0:T(256)S(1)}, f32[256]{0:T(256)}, u32[]{:S(2)}) copy-start(f32[256]{0:T(256)} %param.11) | copy-start | bytes 3076
  282.0 1.4 copy-start.1
  327.2 72.0 %copy-start.17 = (f32[96,768]{1,0:T(8,128)}, f32[96,768]{1,0:T(8,128)S(1)}, u32[]{:S(2)}) copy-start(f32[96,768]{1,0:T(8,128)S(1)} %bitcast_subtract_fusion) | copy-start | bytes 884740
Sparse Core Ops, SparseCore 0:
  11.6 97.6 all-gather.1
  291.3 34.8 reduce-scatter.1
